TPU v7x, 512 devices: a whole 4x4x16 slice. The times are simulated.
512 devices in a mesh: shard: 128 (over z, x, core), rep: 4 (over y).
Axes of the slice: x: 4, y: 4, z: 16, core: 2. Of those that a mesh axis runs over, the one named last changes fastest.
Arguments:
- queries: bfloat16 [512, 32, 128], P(('rep', 'shard')), may hold values from -6 to 6
- passages: bfloat16 [512, 128, 128], P(('shard', 'rep')), may hold values from -0.52734375 to 0.52734375
- labels: int32 [512, 128], P('shard'), may hold values from 0 to 9
- lengths: int32 [512], P('shard'), may hold values from 16 to 128
- candidates: int32 [512, 256], P(('rep', 'shard')), may hold values from 0 to 511, all different within a row
- feedback: int32 [512, 3], P('rep'), may hold values from 0 to 511
- idf: int32 [512, 10], P('rep'), may hold values from 1 to 16
Outputs:
- first_scores: float32 [512, 256], P(('rep', 'shard'))
- final_scores: float32 [512, 256], P(('rep', 'shard'))
Inputs may be any that keep to these rules, and one draw needn't show every extreme that they name: `candidates`: each row names 256 different passages; every passage is named by some row. `feedback`: ids may repeat within a row.
All inputs are finite; a program needn't handle non-finite values.
Results may differ from a plain program's by a relative error of at most 0.0003.
Values may be sent and summed in bfloat16 or wider, within the bound.
A program may use at most 64 MiB of HBM per device.

v0:
```python
import jax
import jax.numpy as jnp
from jax import lax
from jax.sharding import PartitionSpec as P


def normalize(pooled):
    factor = lax.rsqrt(jnp.mean(pooled * pooled, axis=-1, keepdims=True) + 1e-06)
    return (pooled * factor).astype(jnp.bfloat16)


def best_match(vectors, passage_bank, penalty):

    def one_passage(operand):
        document, mask_row = operand
        scores = jnp.einsum("rd,td->rt", vectors, document, preferred_element_type=jnp.float32)
        return jnp.max(scores + mask_row[None, :], axis=1)

    return lax.map(one_passage, (passage_bank, penalty))


def local(queries, passages, labels, lengths, candidates, feedback, idf):
    passage_bank = lax.all_gather(passages, "rep", axis=0, tiled=True)
    local_count = passage_bank.shape[0]
    doc_tokens = passage_bank.shape[1]
    features = queries.shape[2]
    query_tokens = queries.shape[1]
    clusters = idf.shape[1]
    first_passage = lax.axis_index("shard") * local_count
    positions = jnp.arange(doc_tokens, dtype=jnp.int32)
    in_length = positions[None, :] < lengths[:, None]
    penalty = jnp.where(in_length, 0.0, -1000000000.0).astype(jnp.float32)
    cluster_ids = jnp.arange(clusters, dtype=jnp.int32)
    one_hot = ((labels[:, :, None] == cluster_ids[None, None, :]) & in_length[:, :, None]).astype(
        jnp.bfloat16
    )
    cluster_totals = jnp.einsum(
        "ptc,ptd->pcd", one_hot, passage_bank, preferred_element_type=jnp.float32
    )
    passage_ids = first_passage + jnp.arange(local_count, dtype=jnp.int32)
    feedback_counts = jnp.sum(
        (feedback[:, :, None] == passage_ids[None, None, :]).astype(jnp.float32), axis=1
    )
    piece = lax.all_gather(queries, "shard", axis=0, tiled=True)
    number = piece.shape[0]
    best_scores = best_match(piece.reshape(number * query_tokens, features), passage_bank, penalty)
    first_pass = jnp.mean(best_scores.reshape(local_count, number, query_tokens), axis=2).T
    partial_pooled = jnp.einsum(
        "qp,pcd->qcd", feedback_counts, cluster_totals, precision=lax.Precision.HIGHEST
    )
    pooled = lax.psum(partial_pooled, "shard")
    expansion = normalize(pooled)
    weights = idf.astype(jnp.float32) / (8.0 * clusters)
    group_size = expansion.shape[0]
    best_expanded = best_match(
        expansion.reshape(group_size * clusters, features), passage_bank, penalty
    )
    expanded_term = jnp.sum(
        best_expanded.reshape(local_count, group_size, clusters) * weights[None, :, :], axis=2
    ).T
    final_pass = first_pass + expanded_term
    dense_first, dense_final = (
        lax.all_to_all(first_pass, "shard", split_axis=0, concat_axis=1, tiled=True),
        lax.all_to_all(final_pass, "shard", split_axis=0, concat_axis=1, tiled=True),
    )
    first_scores = jnp.take_along_axis(dense_first, candidates, axis=1)
    final_scores = jnp.take_along_axis(dense_final, candidates, axis=1)
    return (first_scores, final_scores)


def solution(mesh):
    return jax.shard_map(
        local,
        mesh=mesh,
        in_specs=(
            P(("rep", "shard"), None, None),
            P(("shard", "rep"), None, None),
            P("shard", None),
            P("shard"),
            P(("rep", "shard"), None),
            P("rep", None),
            P("rep", None),
        ),
        out_specs=(P(("rep", "shard"), None), P(("rep", "shard"), None)),
        check_vma=False,
    )
```

profile of v0, /device:TPU:1, one launch (start us, length us, event | category | flops | bytes accessed | tf_op | source)
XLA Modules:
  0.0 570.7 jit_solution(18290534189307220524)
XLA Ops:
  7.2 0.0 copy-start.3
  7.2 0.0 copy-start.1
  7.2 0.0 copy-start.2
  7.2 0.0 all-reduce.2.cloned.1.call-start
  7.2 10.7 %all_gather.6 = bf16[4,128,128]{2,1,0:T(8,128)(2,1)S(1)} all-gather(bf16[1,128,128]{2,1,0:T(8,128)(2,1)} %param.14), channel_id=1, replica_groups=mesh['shard'=128,'rep'=4] {'rep'}, dimensions={0}, use_global_device_ids=true | all-gather | bytes 163840 | tf_op jit(solution)/shard_map/all_gather | solution.py:23
  17.9 0.7 iota_compare_fusion.1
  18.6 0.8 convert_reduce_fusion
  19.4 0.8 fusion.9
  20.2 1.6 fusion.11
  21.8 0.0 all-reduce.2.cloned.1.call-update
  21.8 0.0 all-gather.2.cloned.1.call-start
  21.9 0.7 all-gather.2.cloned.1.call-update
  22.6 0.0 copy-done.1
  22.6 0.1 copy.23
  22.7 0.0 copy-done.2
  22.8 0.0 copy-done.3
  22.8 0.1 broadcast_select_fusion
  22.8 346.4 %all-reduce.2.cloned.1.call-done = f32[128,10,128]{2,0,1:T(8,128)} async-done(((f32[128,10,128]{2,0,1:T(8,128)}), f32[128,10,128]{2,0,1:T(8,128)}) %all-reduce.2.cloned.1.call-update) | async-done | bytes 655376 | tf_op jit(solution)/shard_map/psum | solution.py:51
  369.2 0.0 copy-start
  369.2 1.4 multiply_reduce_fusion
  370.7 0.0 copy-done
  370.7 0.2 multiply_convert_fusion
  370.9 0.2 copy.22
  371.1 0.1 reshape.82
  371.3 1.7 while.21
  371.3 0.3 fusion.31
  371.6 0.1 dynamic_update_slice.11
  371.7 0.3 fusion.31
  372.0 0.1 dynamic_update_slice.11
  372.1 0.3 fusion.31
  372.4 0.1 dynamic_update_slice.11
  372.5 0.3 fusion.31
  372.8 0.1 dynamic_update_slice.11
  372.9 0.2 reshape.83
  373.2 0.1 multiply_reduce_fusion.1
  373.3 130.1 %all-gather.2.cloned.1.call-done = bf16[128,32,128]{2,1,0:T(8,128)(2,1)} async-done(((bf16[1,32,128]{2,1,0:T(8,128)(2,1)}), bf16[128,32,128]{2,1,0:T(8,128)(2,1)}) %all-gather.2.cloned.1.call-update) | async-done | bytes 1048592 | tf_op jit(solution)/shard_map/all_gather | solution.py:44
  503.5 7.8 %while.20 = (s32[]{:T(128)}, f32[4,4096]{1,0:T(4,128)S(1)}, bf16[4,128,128]{2,1,0:T(8,128)(2,1)S(1)}, bf16[4096,128]{1,0:T(8,128)(2,1)}, f32[4,128]{1,0:T(4,128)S(1)}, /*index=5*/s32[]{:T(128)}, s32[]{:T(128)}) while((s32[]{:T(128)}, f32[4,4096]{1,0:T(4,128)S(1)}, bf16[4,128,128]{2,1,0:T(8,128)(2,1)S(1)}, bf16[4096,128]{1,0:T(8,128)(2,1)}, ...), condition=%wide.region_2.3_spmd, body=%wide.region_0.0_spmd.sunk | while | flops 135262208 | bytes 1132121 | solution.py:19
  503.5 1.7 fusion.28
  505.1 0.2 dynamic_update_slice.10
  505.4 1.7 fusion.28
  507.1 0.2 dynamic_update_slice.10
  507.4 1.7 fusion.28
  509.1 0.2 dynamic_update_slice.10
  509.4 1.7 fusion.28
  511.0 0.2 dynamic_update_slice.10
  511.3 0.1 reshape.81
  511.4 0.1 reduce_sum.36
  511.6 0.7 copy.24
  512.3 10.7 %all-to-all-start.1 = ((f32[128,1,4]{2,1,0:T(1,128)}), f32[128,1,4]{2,1,0:T(1,128)S(1)}, u32[]{:S(2)}, u32[]{:S(2)}) async-start(f32[128,1,4]{2,1,0:T(1,128)} %copy.24), calls=%async_computation.1 | async-start | bytes 131072 | tf_op jit(solution)/shard_map/all_to_all | solution.py:64
  523.0 0.7 copy.20
  523.7 14.1 %all-to-all-done.1 = f32[128,1,4]{2,1,0:T(1,128)S(1)} async-done(((f32[128,1,4]{2,1,0:T(1,128)}), f32[128,1,4]{2,1,0:T(1,128)S(1)}, u32[]{:S(2)}, u32[]{:S(2)}) %all-to-all-start.1) | async-done | bytes 2080 | tf_op jit(solution)/shard_map/all_to_all | solution.py:64
  537.9 5.6 all-to-all-start
  543.5 0.5 broadcast.62
  544.0 0.8 reduce.9
  544.9 0.1 reshape.112
  545.0 13.5 %all-to-all-done = f32[128,1,4]{2,1,0:T(1,128)S(1)} async-done(((f32[128,1,4]{2,1,0:T(1,128)}), f32[128,1,4]{2,1,0:T(1,128)S(1)}, u32[]{:S(2)}, u32[]{:S(2)}) %all-to-all-start) | async-done | bytes 2080 | tf_op jit(solution)/shard_map/all_to_all | solution.py:63
  558.5 0.8 reduce.8
  559.3 0.1 reshape.107
  559.4 1.9 gather_fusion.1
  561.4 1.9 gather_fusion
  563.3 0.6 broadcast_select_fusion.1
  (21 shorter events, 0.1 us)
Async XLA Ops:
  7.2 15.6 %copy-start.3 = (s32[4]{0:T(128)S(1)}, s32[4]{0:T(128)}, u32[]{:S(2)}) copy-start(s32[4]{0:T(128)} %param.16) | copy-start | bytes 52
  7.2 15.4 %copy-start.1 = (s32[128,10]{0,1:T(8,128)S(1)}, s32[128,10]{0,1:T(8,128)}, u32[]{:S(2)}) copy-start(s32[128,10]{0,1:T(8,128)} %param.19) | copy-start | bytes 15364
  7.2 15.6 %copy-start.2 = (s32[1,256]{1,0:T(1,128)S(1)}, s32[1,256]{1,0:T(1,128)}, u32[]{:S(2)}) copy-start(s32[1,256]{1,0:T(1,128)} %param.17) | copy-start | bytes 3076
  7.2 362.0 %all-reduce.2.cloned.1.call-start = ((), (), s32[]{:S(2)}) async-start(), calls=%async_computation.3 | async-start | bytes 1310720 | tf_op jit(solution)/shard_map/psum | solution.py:51
  21.8 481.6 %all-gather.2.cloned.1.call-start = ((), (), s32[]{:S(2)}) async-start(), calls=%async_computation.2 | async-start | bytes 1056768 | tf_op jit(solution)/shard_map/all_gather | solution.py:44
  369.2 1.4 copy-start
  512.3 25.5 %all-to-all-start.1 = ((f32[128,1,4]{2,1,0:T(1,128)}), f32[128,1,4]{2,1,0:T(1,128)S(1)}, u32[]{:S(2)}, u32[]{:S(2)}) async-start(f32[128,1,4]{2,1,0:T(1,128)} %copy.24), calls=%async_computation.1 | async-start | bytes 131072 | tf_op jit(solution)/shard_map/all_to_all | solution.py:64
  537.9 20.6 %all-to-all-start = ((f32[128,1,4]{2,1,0:T(1,128)}), f32[128,1,4]{2,1,0:T(1,128)S(1)}, u32[]{:S(2)}, u32[]{:S(2)}) async-start(f32[128,1,4]{2,1,0:T(1,128)} %copy.20), calls=%async_computation | async-start | bytes 131072 | tf_op jit(solution)/shard_map/all_to_all | solution.py:63
Sparse Core Ops, SparseCore 0:
  22.0 347.2 all-reduce.1
  372.2 131.2 all-gather.1
where the time goes:
time: 571 us
  waiting for transfers between devices  505 us (88%)
  starting transfers between devices  16.4 us (3%)
  between operations  14.3 us (3%)
  blocking collectives  10.7 us (2%)
  matrix products  10.2 us (2%)
  local copies, waits for them, and re-layouts  8.35 us (1%)
    psum x1, waiting for transfers between devices, local(): pooled = lax.psum(partial_pooled, 'shard')  346 us
    all_gather x1, waiting for transfers between devices, local(): piece = lax.all_gather(queries, 'shard', axis=0, tiled=True)  130 us
    all_to_all x1, waiting for transfers between devices, local(): lax.all_to_all(final_pass, 'shard', split_axis=0, concat_axis=1, tiled=True)  14.1 us
    all_to_all x1, waiting for transfers between devices, local(): lax.all_to_all(first_pass, 'shard', split_axis=0, concat_axis=1, tiled=True)  13.5 us
  transfers between devices with their start and end apart: 4, of which 4 were waited for; matrix products, arithmetic and copies ran while one was open for 1% of the time, Pallas kernels for 0%

commit v1 on v0

v1 whole, which is shorter than its diff:
```python
import functools

import jax
import jax.numpy as jnp
from jax import lax
from jax.experimental import pallas as pl
from jax.experimental.pallas import tpu as pltpu
from jax.sharding import PartitionSpec as P

MESH = pl.DeviceIdType.MESH
F32 = jnp.float32
BF16 = jnp.bfloat16
NT = (((1,), (1,)), ((), ()))

NZ, NX, NY, NC = 16, 4, 4, 2
PLANE = NX * NY * NC
ROW = NX * NC
QTOK, PTOK, D = 32, 128, 128
NCLUS, CPAD, FB = 10, 16, 3
NCAND = 256
WIDE = NCLUS * D
QROWS = PLANE * QTOK
EROWS = PLANE * CPAD
CHUNKS = 2
TILE = 256
RS_ORDER = (8, 7, 9, 6, 10, 5, 11, 4, 12, 3, 13, 2, 14, 1, 15)
RELAYS = (
    (0, ((2, 2), (-2, 14), (1, 1), (-1, 15))),
    (2, ((2, 4), (1, 3))),
    (14, ((-2, 12), (-1, 13))),
    (4, ((2, 6), (1, 5))),
    (12, ((-2, 10), (-1, 11))),
    (6, ((2, 8), (1, 7))),
    (10, ((-1, 9),)),
)


def ring(n):
    return min(n, 4 - n)


OFFSETS = sorted(
    [(dy, dx, dc) for dy in range(NY) for dx in range(NX) for dc in range(NC)][1:],
    key=lambda o: -(ring(o[0]) + ring(o[1])),
)


def iota(shape, dim):
    return lax.broadcasted_iota(jnp.int32, shape, dim)


def split3(a):
    hi = a.astype(BF16)
    rest = a - hi.astype(F32)
    mid = rest.astype(BF16)
    low = (rest - mid.astype(F32)).astype(BF16)
    return hi, mid, low


def kernel(
    q_hbm, p_hbm, lab_hbm, len_ref, cand_hbm, fb_hbm, idf_hbm,
    first_ref, final_ref,
    qbuf, praw, pas, lab, cand, fb, idf, tot, part, rs, es, exb, best, back, ret,
    load_sem, tot_send, tot_recv, query_send, query_recv, pas_send, pas_recv,
    rs_send, rs_recv, exp_send, exp_recv, ret_send, ret_recv, near_sem, far_sem,
):
    s = lax.axis_index("shard")
    y = lax.axis_index("rep")
    core = lax.rem(s, 2)
    x = lax.rem(lax.div(s, 2), NX)
    z = lax.div(s, ROW)

    def device(dz=0, dy=0, dx=0, dc=0):
        tz = lax.rem(z + (dz + NZ), NZ)
        ty = lax.rem(y + (dy + NY), NY)
        tx = lax.rem(x + (dx + NX), NX)
        tc = lax.rem(core + dc, 2)
        return ((tz * NX + tx) * NC + tc, ty)

    def remote(src, dst, send, recv, to):
        return pltpu.make_async_remote_copy(
            src_ref=src, dst_ref=dst, send_sem=send, recv_sem=recv, device_id=to, device_id_type=MESH
        )

    row_steps = [(dx, dc) for dx in (2, 1, 3, 0) for dc in (0, 1) if (dx, dc) != (0, 0)]
    barrier = pltpu.get_barrier_semaphore()
    near = [device(dx=dx, dc=dc) for dx, dc in row_steps]
    near += [device(dy=dy) for dy in (2, 1, 3)]
    near += [device(dz=dz) for dz in (2, -2, 1, -1)]
    for to in near:
        pl.semaphore_signal(barrier, inc=1, device_id=to, device_id_type=MESH)

    loads = [
        pltpu.make_async_copy(src, dst, load_sem.at[i])
        for i, (src, dst) in enumerate(
            (
                (p_hbm.at[0], praw),
                (lab_hbm, lab),
                (q_hbm.at[0], qbuf.at[0, 0]),
                (idf_hbm, idf),
                (fb_hbm, fb),
                (cand_hbm, cand),
            )
        )
    ]
    for copy in loads:
        copy.start()

    length = len_ref[y]
    loads[0].wait()
    loads[1].wait()
    passage = praw[...]
    labels = lab[pl.ds(y, 1), :]
    picked = (iota((CPAD, PTOK), 0) == labels) & (iota((CPAD, PTOK), 1) < length)
    totals = jnp.dot(
        jnp.where(picked, 1.0, 0.0).astype(BF16), passage, preferred_element_type=F32
    )
    for c in range(NCLUS):
        tot[0, 0:1, c * D : (c + 1) * D] = totals[c : c + 1, :]
    wide = passage.astype(F32)
    masked = jnp.where(iota((PTOK, D), 0) < length, wide, wide[0:1, :])
    pas[0] = masked.astype(BF16)
    loads[2].wait()
    loads[3].wait()
    tot[0, 0:1, WIDE : WIDE + D] = jnp.zeros((1, D), F32)
    mine = jnp.where(iota((8, NZ * ROW), 1) == s, 1.0, 0.0).astype(BF16)
    weights = lax.dot_general(mine, idf[...].astype(F32).astype(BF16), NT, preferred_element_type=F32)
    tot[0, 0:1, WIDE : WIDE + NCLUS] = weights[0:1, :]
    back[...] = jnp.zeros_like(back)

    pl.semaphore_wait(barrier, len(near))

    sends = []

    def go(copy):
        copy.start()
        sends.append(copy)

    for dz in (2, -2):
        pl.semaphore_signal(near_sem, inc=1, device_id=device(dz=dz), device_id_type=MESH)

    def pass_copy(source, slot, dz, chunk):
        rows = pl.ds(chunk * (PTOK // CHUNKS), PTOK // CHUNKS)
        k = slot * CHUNKS + chunk
        return remote(
            pas.at[source, rows], pas.at[slot, rows], pas_send.at[k], pas_recv.at[k], device(dz=dz)
        )

    def pass_wait(slot, chunk):
        pass_copy(slot, slot, 1, chunk).wait_recv()

    def relay(entry):
        source, hops = entry
        for chunk in range(CHUNKS):
            if source:
                pass_wait(source, chunk)
            for dz, slot in hops:
                go(pass_copy(source, slot, dz, chunk))

    row_tot, row_query = [], []
    for dx, dc in row_steps:
        slot = dx * NC + dc
        copy = remote(
            tot.at[0, pl.ds(0, 1)], tot.at[0, pl.ds(slot, 1)],
            tot_send.at[slot], tot_recv.at[slot], device(dx=dx, dc=dc),
        )
        go(copy)
        row_tot.append(copy)
    relay(RELAYS[0])
    for dx, dc in row_steps:
        slot = dx * NC + dc
        copy = remote(
            qbuf.at[0, 0], qbuf.at[0, slot],
            query_send.at[slot], query_recv.at[slot], device(dx=dx, dc=dc),
        )
        go(copy)
        row_query.append(copy)

    loads[4].wait()
    loads[5].wait()
    turn = lax.rem(iota((NZ, NZ * ROW), 0) + z, NZ) * ROW + (x * NC + core)
    pick = jnp.where(iota((NZ, NZ * ROW), 1) == turn, 1.0, 0.0).astype(F32)
    ids = lax.dot_general(
        pick, fb[...].astype(F32), NT,
        precision=lax.Precision.HIGHEST, preferred_element_type=F32,
    )
    slots = iota((NZ, PLANE), 1)
    slot_y = lax.rem(y + NY - lax.div(slots, ROW), NY)
    slot_x = lax.rem(x + NX - lax.rem(lax.div(slots, NC), NX), NX)
    slot_c = lax.rem(core + lax.rem(slots, NC), 2)
    slot_id = (z * PLANE + slot_x * (NC * NY) + slot_c * NY + slot_y).astype(F32)
    counts = jnp.zeros((NZ, PLANE), F32)
    for k in range(FB):
        counts += jnp.where(jnp.abs(slot_id - ids[:, k : k + 1]) < 0.5, 1.0, 0.0)
    counts = counts.astype(BF16)

    for copy in row_tot:
        copy.wait_recv()
    col_tot, col_query = [], []
    for dy in (2, 1, 3):
        copy = remote(
            tot.at[0], tot.at[dy], tot_send.at[ROW + dy], tot_recv.at[ROW + dy], device(dy=dy)
        )
        go(copy)
        col_tot.append(copy)
    pl.semaphore_wait(near_sem, 2)
    for dz in (4, -4):
        pl.semaphore_signal(far_sem, inc=1, device_id=device(dz=dz), device_id_type=MESH)
    for copy in row_query:
        copy.wait_recv()
    for dy in (2, 1, 3):
        copy = remote(
            qbuf.at[0], qbuf.at[dy],
            query_send.at[ROW + dy], query_recv.at[ROW + dy], device(dy=dy),
        )
        go(copy)
        col_query.append(copy)
    relay(RELAYS[1])
    relay(RELAYS[2])
    for copy in col_tot:
        copy.wait_recv()

    table = tot[...].reshape(PLANE, WIDE + D)
    summed = None
    for piece in split3(table[:, :WIDE]):
        term = jnp.dot(counts, piece, preferred_element_type=F32)
        summed = term if summed is None else summed + term
    part[...] = summed
    pl.semaphore_wait(far_sem, 2)
    parts = []
    for dz in RS_ORDER:
        copy = remote(
            part.at[pl.ds(dz, 1)], rs.at[pl.ds(dz, 1)],
            rs_send.at[dz], rs_recv.at[dz], device(dz=dz),
        )
        go(copy)
        parts.append(copy)
    rs[0:1, :] = summed[0:1, :]

    owner = lax.div(iota((PLANE, EROWS), 1), CPAD)
    spread = jnp.where(
        lax.rem(iota((D, EROWS), 1), CPAD) == iota((D, EROWS), 0), 1.0, 0.0
    ).astype(BF16)
    idf_rows = jnp.dot(table[:, WIDE:].astype(BF16), spread, preferred_element_type=F32)
    exp_weight = jnp.where(owner == iota((PLANE, EROWS), 0), idf_rows, 0.0).astype(BF16)
    query_weight = jnp.where(
        lax.div(iota((PLANE, QROWS), 1), QTOK) == iota((PLANE, QROWS), 0), 1.0, 0.0
    ).astype(BF16)

    for entry in RELAYS[3:]:
        relay(entry)

    for copy in parts:
        copy.wait_recv()
    pooled = jnp.sum(rs[...], axis=0, keepdims=True)
    es[...] = jnp.zeros_like(es)
    for c in range(NCLUS):
        es[c : c + 1, :] = pooled[:, c * D : (c + 1) * D]
    rows = es[...]
    factor = lax.rsqrt(jnp.mean(rows * rows, axis=1, keepdims=True) + 1e-06)
    exb[0] = (rows * factor).astype(BF16)
    expansions = []
    for dy, dx, dc in OFFSETS:
        slot = dy * ROW + dx * NC + dc
        copy = remote(
            exb.at[0], exb.at[slot], exp_send.at[slot], exp_recv.at[slot],
            device(dy=dy, dx=dx, dc=dc),
        )
        go(copy)
        expansions.append(copy)

    for copy in col_query:
        copy.wait_recv()
    for slot in (1, 15, 3, 13, 5, 11, 7, 9, 8):
        for chunk in range(CHUNKS):
            pass_wait(slot, chunk)

    def maxima(vectors, n):
        scores = lax.dot_general(pas[n], vectors, NT, preferred_element_type=F32)
        return jnp.max(scores, axis=0, keepdims=True)

    for tile in range(QROWS // TILE):
        vectors = qbuf[tile // 1].reshape(ROW * QTOK, D)
        for n in range(NZ):
            best[n : n + 1, tile * TILE : (tile + 1) * TILE] = maxima(vectors, n)

    def reduce(weight, values):
        hi, mid, low = split3(values)
        total = lax.dot_general(weight, hi, NT, preferred_element_type=F32)
        total += lax.dot_general(weight, mid, NT, preferred_element_type=F32)
        return total + lax.dot_general(weight, low, NT, preferred_element_type=F32)

    plain = reduce(query_weight, best[:, :QROWS]) * (1.0 / QTOK)
    back[:, 0:NZ] = plain

    ids = cand[...]
    cand_y = lax.rem(ids, NY)
    cand_c = lax.rem(lax.div(ids, NY), NC)
    cand_x = lax.rem(lax.div(ids, NY * NC), NX)
    cand_z = lax.div(ids, PLANE)
    cand_slot = (
        lax.rem(cand_y + NY - y, NY) * ROW
        + lax.rem(cand_x + NX - x, NX) * NC
        + lax.rem(cand_c + core, 2)
    )
    cand_n = lax.rem(z + NZ - cand_z, NZ)
    slot_hot = jnp.where(iota((PLANE, NCAND), 0) == cand_slot, 1.0, 0.0).astype(BF16)
    n_hot = iota((NZ, NCAND), 0) == cand_n

    for copy in expansions:
        copy.wait_recv()
    for tile in range(EROWS // TILE):
        part_rows = TILE // CPAD
        vectors = exb[tile * part_rows : (tile + 1) * part_rows].reshape(TILE, D)
        for n in range(NZ):
            at = QROWS + tile * TILE
            best[n : n + 1, at : at + TILE] = maxima(vectors, n)
    added = reduce(exp_weight, best[:, QROWS:]) * (1.0 / (8.0 * NCLUS))
    back[:, NZ : 2 * NZ] = plain + added

    returns = []
    for dy, dx, dc in OFFSETS:
        slot = dy * ROW + dx * NC + dc
        copy = remote(
            back.at[pl.ds(slot, 1)], ret.at[pl.ds(slot, 1)],
            ret_send.at[slot], ret_recv.at[slot], device(dy=-dy, dx=-dx, dc=dc),
        )
        go(copy)
        returns.append(copy)
    ret[0:1, :] = back[0:1, :]
    for copy in returns:
        copy.wait_recv()
    flat = ret[...].T[: 2 * NZ, :]
    chosen = None
    for piece in split3(flat):
        term = jnp.dot(piece, slot_hot, preferred_element_type=F32)
        chosen = term if chosen is None else chosen + term
    first_ref[...] = jnp.sum(jnp.where(n_hot, chosen[:NZ], 0.0), axis=0, keepdims=True)
    final_ref[...] = jnp.sum(jnp.where(n_hot, chosen[NZ:], 0.0), axis=0, keepdims=True)
    for copy in sends:
        copy.wait_send()


def local(queries, passages, labels, lengths, candidates, feedback, idf):
    dma = pltpu.SemaphoreType.DMA
    anywhere = pl.BlockSpec(memory_space=pl.ANY)
    return pl.pallas_call(
        kernel,
        out_shape=(
            jax.ShapeDtypeStruct((1, NCAND), F32),
            jax.ShapeDtypeStruct((1, NCAND), F32),
        ),
        in_specs=[anywhere] * 3 + [pl.BlockSpec(memory_space=pltpu.SMEM)] + [anywhere] * 3,
        out_specs=(
            pl.BlockSpec(memory_space=pltpu.VMEM),
            pl.BlockSpec(memory_space=pltpu.VMEM),
        ),
        scratch_shapes=[
            pltpu.VMEM((NY, ROW, QTOK, D), BF16),
            pltpu.VMEM((PTOK, D), BF16),
            pltpu.VMEM((NZ, PTOK, D), BF16),
            pltpu.VMEM((NY, PTOK), jnp.int32),
            pltpu.VMEM((1, NCAND), jnp.int32),
            pltpu.VMEM((FB, NZ * ROW), jnp.int32),
            pltpu.VMEM((NCLUS, NZ * ROW), jnp.int32),
            pltpu.VMEM((NY, ROW, WIDE + D), F32),
            pltpu.VMEM((NZ, WIDE), F32),
            pltpu.VMEM((NZ, WIDE), F32),
            pltpu.VMEM((CPAD, D), F32),
            pltpu.VMEM((PLANE, CPAD, D), BF16),
            pltpu.VMEM((NZ, QROWS + EROWS), F32),
            pltpu.VMEM((PLANE, D), F32),
            pltpu.VMEM((PLANE, D), F32),
            dma((6,)),
            dma((ROW + NY,)), dma((ROW + NY,)),
            dma((ROW + NY,)), dma((ROW + NY,)),
            dma((NZ * CHUNKS,)), dma((NZ * CHUNKS,)),
            dma((NZ,)), dma((NZ,)),
            dma((PLANE,)), dma((PLANE,)),
            dma((PLANE,)), dma((PLANE,)),
            pltpu.SemaphoreType.REGULAR,
            pltpu.SemaphoreType.REGULAR,
        ],
        compiler_params=pltpu.CompilerParams(collective_id=0, has_side_effects=True),
    )(queries, passages, labels, lengths, candidates, feedback.T, idf.T)


def solution(mesh):
    return jax.shard_map(
        local,
        mesh=mesh,
        in_specs=(
            P(("rep", "shard"), None, None),
            P(("shard", "rep"), None, None),
            P("shard", None),
            P("shard"),
            P(("rep", "shard"), None),
            P("rep", None),
            P("rep", None),
        ),
        out_specs=(P(("rep", "shard"), None), P(("rep", "shard"), None)),
        check_vma=False,
    )
```

time: 571 us -> 48.2 us (0.08)
  waiting for transfers between devices: 505 us -> 0 us
  Pallas kernels: 0 us -> 45.4 us
  starting transfers between devices: 16.4 us -> 0 us
  between operations: 14.3 us -> 0.65 us
  blocking collectives: 10.7 us -> 0 us
  matrix products: 10.2 us -> 0 us
  local copies, waits for them, and re-layouts: 8.35 us -> 1.85 us
    psum x1 -> x0, waiting for transfers between devices: 346 us -> none  [local(): pooled = lax.psum(partial_pooled, 'shard')]
    all_gather x1 -> x0, waiting for transfers between devices: 130 us -> none  [local(): piece = lax.all_gather(queries, 'shard', axis=0, tiled=True)]
    pallas_call x0 -> x1, Pallas kernels: none -> 45.4 us  [local(): pl.pallas_call(kernel, out_shape=(jax.ShapeDtypeStruct((1, NCAND), F32),...]
    all_to_all x2 -> x0, waiting for transfers between devices: 27.6 us -> none  [the longest x1 14.1 us: local(): lax.all_to_all(final_pass, 'shard', split_axis=0, concat_axis=1, tiled=True)]
    all_to_all x2 -> x0, starting transfers between devices: 16.3 us -> none  [the longest x1 10.7 us: local(): lax.all_to_all(final_pass, 'shard', split_axis=0, concat_axis=1, tiled=True)]
    all_gather x1 -> x0, blocking collectives: 10.7 us -> none  [local(): passage_bank = lax.all_gather(passages, 'rep', axis=0, tiled=True)]
    dot_general x10 -> x0, matrix products: 10.2 us -> none  [the longest x8 7.74 us: one_passage(): jnp.einsum('rd,td->rt', vectors, document, preferred_element_type=jnp.flo...]
  transfers between devices with their start and end apart: 4 -> 0, of which waited for: 4 -> 0; matrix products, arithmetic and copies ran while one was open for 1% -> 0% of each run, Pallas kernels for 0% -> 0%
where the time goes in v1:
time: 48.2 us; the launch traced here: 47.9 us
  Pallas kernels  45.4 us (94%)
  local copies, waits for them, and re-layouts  1.85 us (4%)
  between operations  0.65 us (1%)
    pallas_call x1, Pallas kernels, local(): pl.pallas_call(kernel, out_shape=(jax.ShapeDtypeStruct((1, NCAND), F32),...  45.4 us
    unnamed x6, local copies, waits for them, and re-layouts  1.85 us

profile of v1, /device:TPU:1, one launch (start us, length us, event | category | flops | bytes accessed | tf_op | source)
XLA Modules:
  0.0 47.9 jit_solution(7576415693609297965)
XLA Ops:
  0.6 45.4 %shard_map.86 = (f32[1,256]{1,0:T(1,128)}, f32[1,256]{1,0:T(1,128)}) custom-call(bf16[1,32,128]{2,1,0:T(8,128)(2,1)} %q_hbm.1, bf16[1,128,128]{2,1,0:T(8,128)(2,1)} %p_hbm.1, s32[4,128]{1,0:T(4,128)} %lab_hbm.1, s32[4]{0:T(128)} %len_ref.1, s32[1,256]{1,0:T(1,128)} %cand_hbm.1, s32[3,128]{1,0:T(4,128)} %bitcast.3, s32[10,128]{1,0:T(8,128)} %bitcast.2), custom_call_target="tpu_custom_call" | custom-call | tf_op jit(solution)/shard_map/pallas_call | solution.py:347
  46.1 0.0 copy-start.1
  46.1 0.7 %copy-done.1 = f32[1,256]{1,0:T(1,128)S(1)} copy-done((f32[1,256]{1,0:T(1,128)S(1)}, f32[1,256]{1,0:T(1,128)}, u32[]{:S(2)}) %copy-start.1) | copy-done | bytes 1048
  46.7 0.0 copy-start
  46.7 0.6 %copy.11 = f32[1,256]{1,0:T(1,128)} copy(f32[1,256]{1,0:T(1,128)S(1)} %copy-done.1) | data formatting | bytes 2048
  47.3 0.1 copy-done
  47.4 0.6 %copy.12 = f32[1,256]{1,0:T(1,128)} copy(f32[1,256]{1,0:T(1,128)S(1)} %copy-done) | data formatting | bytes 2048
Async XLA Ops:
  46.1 0.7 %copy-start.1 = (f32[1,256]{1,0:T(1,128)S(1)}, f32[1,256]{1,0:T(1,128)}, u32[]{:S(2)}) copy-start(f32[1,256]{1,0:T(1,128)} %get-tuple-element.4) | copy-start | bytes 3076
  46.7 0.6 %copy-start = (f32[1,256]{1,0:T(1,128)S(1)}, f32[1,256]{1,0:T(1,128)}, u32[]{:S(2)}) copy-start(f32[1,256]{1,0:T(1,128)} %get-tuple-element.5) | copy-start | bytes 3076

commit v2 on v1

v2 whole, which is shorter than its diff:
```python
import functools

import jax
import jax.numpy as jnp
from jax import lax
from jax.experimental import pallas as pl
from jax.experimental.pallas import tpu as pltpu
from jax.sharding import PartitionSpec as P

MESH = pl.DeviceIdType.MESH
F32 = jnp.float32
BF16 = jnp.bfloat16
NT = (((1,), (1,)), ((), ()))

NZ, NX, NY, NC = 16, 4, 4, 2
PLANE = NX * NY * NC
ROW = NX * NC
QTOK, PTOK, D = 32, 128, 128
NCLUS, CPAD, FB = 10, 16, 3
NCAND = 256
QROWS = PLANE * QTOK
EROWS = PLANE * CPAD
EXP = NZ * CPAD
CHUNKS = 2
TILE = 256
RS_ORDER = (8, 7, 9, 6, 10, 5, 11, 4, 12, 3, 13, 2, 14, 1, 15)
RELAYS = (
    (0, ((2, 2), (-2, 14), (1, 1), (-1, 15))),
    (2, ((2, 4), (1, 3))),
    (14, ((-2, 12), (-1, 13))),
    (4, ((2, 6), (1, 5))),
    (12, ((-2, 10), (-1, 11))),
    (6, ((2, 8), (1, 7))),
    (10, ((-1, 9),)),
)


def ring(n):
    return min(n, 4 - n)


OFFSETS = sorted(
    [(dy, dx, dc) for dy in range(NY) for dx in range(NX) for dc in range(NC)][1:],
    key=lambda o: -(ring(o[0]) + ring(o[1])),
)


def iota(shape, dim):
    return lax.broadcasted_iota(jnp.int32, shape, dim)


def split3(a):
    hi = a.astype(BF16)
    rest = a - hi.astype(F32)
    mid = rest.astype(BF16)
    low = (rest - mid.astype(F32)).astype(BF16)
    return hi, mid, low


def kernel(
    q_hbm, p_hbm, lab_hbm, len_hbm, cand_hbm, fb_hbm, idf_hbm,
    out_ref,
    len_ref, qbuf, praw, pas, lab, cand, fb, idf, tot, mix, part, rs, exb, best, back, ret,
    load_sem, tot_send, row_tot_recv, col_tot_recv, query_send, row_query_recv, col_query_recv,
    pas_send, relay_recv, odd_recv, end_recv, rs_send, rs_recv, exp_send, exp_recv, ret_send, ret_recv, near_sem, far_sem,
):
    s = lax.axis_index("shard")
    y = lax.axis_index("rep")
    core = lax.rem(s, 2)
    x = lax.rem(lax.div(s, 2), NX)
    z = lax.div(s, ROW)

    def device(dz=0, dy=0, dx=0, dc=0):
        tz = lax.rem(z + (dz + NZ), NZ)
        ty = lax.rem(y + (dy + NY), NY)
        tx = lax.rem(x + (dx + NX), NX)
        tc = lax.rem(core + dc, 2)
        return ((tz * NX + tx) * NC + tc, ty)

    def remote(src, dst, send, recv, to):
        return pltpu.make_async_remote_copy(
            src_ref=src, dst_ref=dst, send_sem=send, recv_sem=recv, device_id=to, device_id_type=MESH
        )

    row_steps = [(0, 1), (1, 0), (3, 0), (1, 1), (3, 1), (2, 0), (2, 1)]
    barrier = pltpu.get_barrier_semaphore()
    near = [device(dx=dx, dc=dc) for dx, dc in row_steps]
    near += [device(dy=dy) for dy in (2, 1, 3)]
    near += [device(dz=dz) for dz in (2, -2, 1, -1)]
    for to in near:
        pl.semaphore_signal(barrier, inc=1, device_id=to, device_id_type=MESH)

    loads = [
        pltpu.make_async_copy(src, dst, load_sem.at[i])
        for i, (src, dst) in enumerate(
            (
                (p_hbm.at[0], praw),
                (lab_hbm, lab),
                (q_hbm.at[0], qbuf.at[0]),
                (idf_hbm, idf),
                (fb_hbm, fb),
                (cand_hbm, cand),
                (len_hbm, len_ref),
            )
        )
    ]
    for copy in loads:
        copy.start()

    loads[6].wait()
    length = len_ref[y]
    loads[1].wait()
    loads[0].wait()
    passage = praw[...]
    labels = lab[pl.ds(y, 1), :]
    picked = (iota((CPAD, PTOK), 0) == labels) & (iota((CPAD, PTOK), 1) < length)
    totals = jnp.dot(
        jnp.where(picked, 1.0, 0.0).astype(BF16), passage, preferred_element_type=F32
    )
    wide = passage.astype(F32)
    masked = jnp.where(iota((PTOK, D), 0) < length, wide, wide[0:1, :])
    pas[0] = masked.astype(BF16)
    loads[2].wait()
    loads[3].wait()
    mine = jnp.where(
        (iota((CPAD, NZ * ROW), 1) == s) & (iota((CPAD, NZ * ROW), 0) == NCLUS), 1.0, 0.0
    ).astype(BF16)
    spread = jnp.where(
        iota((NCLUS, D), 0) == iota((NCLUS, D), 1), 1.0, 0.0
    ).astype(BF16)
    table = lax.dot_general(
        idf[...].astype(F32).astype(BF16), spread, (((0,), (0,)), ((), ())),
        preferred_element_type=F32,
    ).astype(BF16)
    tot[0] = totals + jnp.dot(mine, table, preferred_element_type=F32)
    back[...] = jnp.zeros_like(back)
    exb[...] = jnp.zeros_like(exb)

    pl.semaphore_wait(barrier, len(near))

    def arrive(ref, sem):
        remote(ref, ref, sem, sem, device(dc=1)).wait_recv()

    def leave(ref, sem):
        remote(ref, ref, sem, sem, device(dc=1)).wait_send()

    for dz in (2, -2):
        pl.semaphore_signal(near_sem, inc=1, device_id=device(dz=dz), device_id_type=MESH)

    def place(slot):
        return slot // 2 + (slot % 2) * (NZ // 2)

    def pass_rows(slot, chunk):
        return pas.at[place(slot), pl.ds(chunk * (PTOK // CHUNKS), PTOK // CHUNKS)]

    def pass_recv(slot, chunk):
        if slot % 2:
            return odd_recv
        return end_recv if slot == NZ // 2 else relay_recv.at[place(slot) * CHUNKS + chunk]

    def relay(entry):
        source, hops = entry
        for chunk in range(CHUNKS):
            if source:
                arrive(pass_rows(source, chunk), pass_recv(source, chunk))
            for dz, slot in hops:
                remote(
                    pass_rows(source, chunk), pass_rows(slot, chunk),
                    pas_send, pass_recv(slot, chunk), device(dz=dz),
                ).start()

    sent = pl.ds(0, NCLUS + 1)
    for dx, dc in row_steps:
        slot = dx * NC + dc
        remote(
            tot.at[0, sent], tot.at[slot, sent], tot_send, row_tot_recv.at[slot], device(dx=dx, dc=dc)
        ).start()

    def col_send(slot):
        for dy in (2, 1, 3):
            remote(
                tot.at[slot, sent], tot.at[dy * ROW + slot, sent],
                tot_send, col_tot_recv, device(dy=dy),
            ).start()

    col_send(0)
    relay(RELAYS[0])
    loads[4].wait()
    loads[5].wait()
    turn = lax.rem(iota((NZ, NZ * ROW), 0) + z, NZ) * ROW + (x * NC + core)
    pick = jnp.where(iota((NZ, NZ * ROW), 1) == turn, 1.0, 0.0).astype(F32)
    ids = lax.dot_general(
        pick, fb[...].astype(F32), NT,
        precision=lax.Precision.HIGHEST, preferred_element_type=F32,
    )
    slots = iota((NZ, PLANE), 1)
    slot_y = lax.rem(y + NY - lax.div(slots, ROW), NY)
    slot_x = lax.rem(x + NX - lax.rem(lax.div(slots, NC), NX), NX)
    slot_c = lax.rem(core + lax.rem(slots, NC), 2)
    slot_id = (z * PLANE + slot_x * (NC * NY) + slot_c * NY + slot_y).astype(F32)
    counts = jnp.zeros((NZ, PLANE), F32)
    for k in range(FB):
        counts += jnp.where(jnp.abs(slot_id - ids[:, k : k + 1]) < 0.5, 1.0, 0.0)
    up = jnp.where(lax.div(iota((EXP, NZ), 0), CPAD) == iota((EXP, NZ), 1), 1.0, 0.0).astype(BF16)
    over = jnp.where(
        lax.div(iota((PLANE, EROWS), 1), CPAD) == iota((PLANE, EROWS), 0), 1.0, 0.0
    ).astype(BF16)
    tall = jnp.dot(up, counts.astype(BF16), preferred_element_type=F32).astype(BF16)
    counts = jnp.dot(tall, over, preferred_element_type=F32)
    same = lax.rem(iota((EXP, EROWS), 0), CPAD) == lax.rem(iota((EXP, EROWS), 1), CPAD)
    mix[...] = jnp.where(same, counts, 0.0).astype(BF16)

    for dx, dc in row_steps:
        slot = dx * NC + dc
        arrive(tot.at[slot, sent], row_tot_recv.at[slot])
        col_send(slot)
    for dx, dc in row_steps:
        slot = dx * NC + dc
        remote(
            qbuf.at[0], qbuf.at[slot], query_send, row_query_recv, device(dx=dx, dc=dc)
        ).start()
    pl.semaphore_wait(near_sem, 2)
    for dz in (4, -4):
        pl.semaphore_signal(far_sem, inc=1, device_id=device(dz=dz), device_id_type=MESH)
    relay(RELAYS[1])
    relay(RELAYS[2])
    arrive(tot.at[pl.ds(ROW, PLANE - ROW), sent], col_tot_recv)

    table = jnp.where(iota((PLANE, CPAD, D), 1) < NCLUS, tot[...], 0.0).reshape(EROWS, D)
    counts = mix[...]
    summed = None
    for piece in split3(table):
        term = jnp.dot(counts, piece, preferred_element_type=F32)
        summed = term if summed is None else summed + term
    part[...] = summed.reshape(NZ, CPAD, D)
    pl.semaphore_wait(far_sem, 2)
    for dz in RS_ORDER:
        remote(
            part.at[dz, pl.ds(0, NCLUS)], rs.at[dz, pl.ds(0, NCLUS)],
            rs_send, rs_recv, device(dz=dz),
        ).start()
    arrive(qbuf.at[pl.ds(1, ROW - 1)], row_query_recv)
    for dy in (2, 1, 3):
        remote(
            qbuf.at[pl.ds(0, ROW)], qbuf.at[pl.ds(dy * ROW, ROW)],
            query_send, col_query_recv, device(dy=dy),
        ).start()

    owner = lax.div(iota((PLANE, EROWS), 1), CPAD)
    spread = jnp.where(
        lax.rem(iota((D, EROWS), 1), CPAD) == iota((D, EROWS), 0), 1.0, 0.0
    ).astype(BF16)
    idf_rows = tot[:, NCLUS].astype(BF16)
    idf_rows = jnp.dot(idf_rows, spread, preferred_element_type=F32)
    exp_weight = jnp.where(owner == iota((PLANE, EROWS), 0), idf_rows, 0.0).astype(BF16)
    query_weight = jnp.where(
        lax.div(iota((PLANE, QROWS), 1), QTOK) == iota((PLANE, QROWS), 0), 1.0, 0.0
    ).astype(BF16)

    for entry in RELAYS[3:]:
        relay(entry)

    arrive(rs.at[pl.ds(1, NZ - 1), pl.ds(0, NCLUS)], rs_recv)
    rows = part[0, 0:NCLUS]
    for dz in range(1, NZ):
        rows += rs[dz, 0:NCLUS]
    factor = lax.rsqrt(jnp.mean(rows * rows, axis=1, keepdims=True) + 1e-06)
    exb[0, 0:NCLUS] = (rows * factor).astype(BF16)
    for dy, dx, dc in OFFSETS:
        slot = dy * ROW + dx * NC + dc
        remote(
            exb.at[0, pl.ds(0, NCLUS)], exb.at[slot, pl.ds(0, NCLUS)], exp_send, exp_recv,
            device(dy=dy, dx=dx, dc=dc),
        ).start()

    arrive(qbuf.at[pl.ds(ROW, PLANE - ROW)], col_query_recv)
    arrive(pas.at[pl.ds(NZ // 2, NZ // 2)], odd_recv)
    arrive(pas.at[NZ // 4], end_recv)

    def maxima(vectors, n):
        scores = lax.dot_general(pas[n], vectors, NT, preferred_element_type=F32)
        return jnp.max(scores, axis=0, keepdims=True)

    for tile in range(QROWS // TILE):
        vectors = qbuf[tile * ROW : (tile + 1) * ROW].reshape(TILE, D)
        for n in range(NZ):
            best[n : n + 1, tile * TILE : (tile + 1) * TILE] = maxima(vectors, n)

    def reduce(weight, values):
        hi, mid, low = split3(values)
        total = lax.dot_general(weight, hi, NT, preferred_element_type=F32)
        total += lax.dot_general(weight, mid, NT, preferred_element_type=F32)
        return total + lax.dot_general(weight, low, NT, preferred_element_type=F32)

    plain = reduce(query_weight, best[:, :QROWS]) * (1.0 / QTOK)
    back[:, 0:NZ] = plain

    ids = cand[...]
    cand_y = lax.rem(ids, NY)
    cand_c = lax.rem(lax.div(ids, NY), NC)
    cand_x = lax.rem(lax.div(ids, NY * NC), NX)
    cand_z = lax.div(ids, PLANE)
    cand_slot = (
        lax.rem(cand_y + NY - y, NY) * ROW
        + lax.rem(cand_x + NX - x, NX) * NC
        + lax.rem(cand_c + core, 2)
    )
    cand_n = lax.rem(z + NZ - cand_z, NZ)
    cand_n = lax.div(cand_n, 2) + lax.rem(cand_n, 2) * (NZ // 2)
    slot_hot = jnp.where(iota((PLANE, NCAND), 0) == cand_slot, 1.0, 0.0).astype(BF16)
    n_hot = iota((NZ, NCAND), 0) == cand_n

    arrive(exb.at[pl.ds(1, PLANE - 1), pl.ds(0, NCLUS)], exp_recv)
    for tile in range(EROWS // TILE):
        part_rows = TILE // CPAD
        vectors = exb[tile * part_rows : (tile + 1) * part_rows].reshape(TILE, D)
        for n in range(NZ):
            at = QROWS + tile * TILE
            best[n : n + 1, at : at + TILE] = maxima(vectors, n)
    added = reduce(exp_weight, best[:, QROWS:]) * (1.0 / (8.0 * NCLUS))
    back[:, NZ : 2 * NZ] = plain + added

    for dy, dx, dc in OFFSETS:
        slot = dy * ROW + dx * NC + dc
        remote(
            back.at[pl.ds(slot, 1)], ret.at[pl.ds(slot, 1)], ret_send, ret_recv,
            device(dy=-dy, dx=-dx, dc=dc),
        ).start()
    ret[0:1, :] = back[0:1, :]
    others = pl.ds(1, PLANE - 1)
    leave(tot.at[others, sent], tot_send)
    leave(qbuf.at[others], query_send)
    leave(pas.at[pl.ds(1, NZ - 1)], pas_send)
    leave(rs.at[pl.ds(1, NZ - 1), pl.ds(0, NCLUS)], rs_send)
    leave(exb.at[others, pl.ds(0, NCLUS)], exp_send)
    arrive(ret.at[others], ret_recv)
    flat = ret[...].T[: 2 * NZ, :]
    chosen = None
    for piece in split3(flat):
        term = jnp.dot(piece, slot_hot, preferred_element_type=F32)
        chosen = term if chosen is None else chosen + term
    out_ref[0:1, :] = jnp.sum(jnp.where(n_hot, chosen[:NZ], 0.0), axis=0, keepdims=True)
    out_ref[1:2, :] = jnp.sum(jnp.where(n_hot, chosen[NZ:], 0.0), axis=0, keepdims=True)
    leave(ret.at[others], ret_send)


def local(queries, passages, labels, lengths, candidates, feedback, idf):
    dma = pltpu.SemaphoreType.DMA
    anywhere = pl.BlockSpec(memory_space=pl.ANY)
    scores = pl.pallas_call(
        kernel,
        out_shape=jax.ShapeDtypeStruct((2, NCAND), F32),
        in_specs=[anywhere] * 7,
        out_specs=pl.BlockSpec(memory_space=pltpu.VMEM),
        scratch_shapes=[
            pltpu.SMEM((NY,), jnp.int32),
            pltpu.VMEM((PLANE, QTOK, D), BF16),
            pltpu.VMEM((PTOK, D), BF16),
            pltpu.VMEM((NZ, PTOK, D), BF16),
            pltpu.VMEM((NY, PTOK), jnp.int32),
            pltpu.VMEM((1, NCAND), jnp.int32),
            pltpu.VMEM((FB, NZ * ROW), jnp.int32),
            pltpu.VMEM((NCLUS, NZ * ROW), jnp.int32),
            pltpu.VMEM((PLANE, CPAD, D), F32),
            pltpu.VMEM((EXP, EROWS), BF16),
            pltpu.VMEM((NZ, CPAD, D), F32),
            pltpu.VMEM((NZ, CPAD, D), F32),
            pltpu.VMEM((PLANE, CPAD, D), BF16),
            pltpu.VMEM((NZ, QROWS + EROWS), F32),
            pltpu.VMEM((PLANE, D), F32),
            pltpu.VMEM((PLANE, D), F32),
            dma((7,)),
            dma, dma((ROW,)), dma,
            dma, dma, dma,
            dma, dma((NZ * CHUNKS // 2,)), dma, dma,
            dma, dma,
            dma, dma,
            dma, dma,
            pltpu.SemaphoreType.REGULAR,
            pltpu.SemaphoreType.REGULAR,
        ],
        compiler_params=pltpu.CompilerParams(collective_id=0, has_side_effects=True),
    )(queries, passages, labels, lengths, candidates, feedback.T, idf.T)
    return scores[0:1], scores[1:2]


def solution(mesh):
    return jax.shard_map(
        local,
        mesh=mesh,
        in_specs=(
            P(("rep", "shard"), None, None),
            P(("shard", "rep"), None, None),
            P("shard", None),
            P("shard"),
            P(("rep", "shard"), None),
            P("rep", None),
            P("rep", None),
        ),
        out_specs=(P(("rep", "shard"), None), P(("rep", "shard"), None)),
        check_vma=False,
    )
```

time: 48.2 us -> 43.7 us (0.907)
  Pallas kernels: 45.4 us -> 41.5 us
  local copies, waits for them, and re-layouts: 1.85 us -> 1.32 us
    pallas_call x1, Pallas kernels: 45.4 us -> 41.5 us  [local(): pl.pallas_call(kernel, out_shape=jax.ShapeDtypeStruct((2, NCAND), F32), i...]
    unnamed x6 -> x0, local copies, waits for them, and re-layouts: 1.85 us -> none
    slice x0 -> x1, local copies, waits for them, and re-layouts: none -> 1.32 us  [local(): return (scores[0:1], scores[1:2])]
where the time goes in v2:
time: 43.7 us; the launch traced here: 43.5 us
  Pallas kernels  41.5 us (95%)
  local copies, waits for them, and re-layouts  1.32 us (3%)
  between operations  0.64 us (1%)
    pallas_call x1, Pallas kernels, local(): pl.pallas_call(kernel, out_shape=jax.ShapeDtypeStruct((2, NCAND), F32), i...  41.5 us
    slice x1, local copies, waits for them, and re-layouts, local(): return (scores[0:1], scores[1:2])  1.32 us

profile of v2, /device:TPU:1, one launch (start us, length us, event | category | flops | bytes accessed | tf_op | source)
XLA Modules:
  0.0 43.5 jit_solution(405393186205237766)
XLA Ops:
  0.6 41.5 %shard_map.86 = f32[2,256]{1,0:T(2,128)} custom-call(bf16[1,32,128]{2,1,0:T(8,128)(2,1)} %q_hbm.1, bf16[1,128,128]{2,1,0:T(8,128)(2,1)} %p_hbm.1, s32[4,128]{1,0:T(4,128)} %lab_hbm.1, s32[4]{0:T(128)} %len_hbm.1, s32[1,256]{1,0:T(1,128)} %cand_hbm.1, s32[3,128]{1,0:T(4,128)} %bitcast.3, s32[10,128]{1,0:T(8,128)} %bitcast.2), custom_call_target="tpu_custom_call" | custom-call | tf_op jit(solution)/shard_map/pallas_call | solution.py:350
  42.2 1.3 %fusion = (f32[1,256]{1,0:T(1,128)}, f32[1,256]{1,0:T(1,128)}) fusion(f32[2,256]{1,0:T(2,128)} %shard_map.86), kind=kLoop, calls=%fused_computation | loop fusion | bytes 4096 | tf_op jit(solution)/shard_map/slice | solution.py:384

commit v3 on v2

--- a/solution.py
+++ b/solution.py
@@ -17,12 +17,13 @@
 ROW = NX * NC
 QTOK, PTOK, D = 32, 128, 128
 NCLUS, CPAD, FB = 10, 16, 3
+TROWS = NCLUS + 1
 NCAND = 256
 QROWS = PLANE * QTOK
-EROWS = PLANE * CPAD
-EXP = NZ * CPAD
-CHUNKS = 2
+EROWS = PLANE * NCLUS
+EXP = NZ * NCLUS
 TILE = 256
+GROUP = 4
 RS_ORDER = (8, 7, 9, 6, 10, 5, 11, 4, 12, 3, 13, 2, 14, 1, 15)
 RELAYS = (
     (0, ((2, 2), (-2, 14), (1, 1), (-1, 15))),
@@ -49,6 +50,14 @@
     return lax.broadcasted_iota(jnp.int32, shape, dim)
 
 
+def tenth(a):
+    return lax.shift_right_logical(a * 6554, 16)
+
+
+def eleventh(a):
+    return lax.shift_right_logical(a * 5958, 16)
+
+
 def split3(a):
     hi = a.astype(BF16)
     rest = a - hi.astype(F32)
@@ -60,9 +69,9 @@
 def kernel(
     q_hbm, p_hbm, lab_hbm, len_hbm, cand_hbm, fb_hbm, idf_hbm,
     out_ref,
-    len_ref, qbuf, praw, pas, lab, cand, fb, idf, tot, mix, part, rs, exb, best, back, ret,
-    load_sem, tot_send, row_tot_recv, col_tot_recv, query_send, row_query_recv, col_query_recv,
-    pas_send, relay_recv, odd_recv, end_recv, rs_send, rs_recv, exp_send, exp_recv, ret_send, ret_recv, near_sem, far_sem,
+    len_ref, qbuf, praw, pas, lab, cand, fb, idf, tot, mix, part, rs, exb, best, best_exp, back, ret,
+    load_sem, tot_send, tot_recv, query_send, row_query_recv, col_query_recv,
+    pas_send, relay_recv, odd_recv, end_recv, rs_send, rs_recv, exp_send, exp_recv, ret_send, ret_recv, near_sem, far_sem, plane_sem,
 ):
     s = lax.axis_index("shard")
     y = lax.axis_index("rep")
@@ -82,11 +91,12 @@
             src_ref=src, dst_ref=dst, send_sem=send, recv_sem=recv, device_id=to, device_id_type=MESH
         )
 
-    row_steps = [(0, 1), (1, 0), (3, 0), (1, 1), (3, 1), (2, 0), (2, 1)]
+    row_steps = [(2, 0), (2, 1), (1, 0), (3, 0), (1, 1), (3, 1), (0, 1)]
     barrier = pltpu.get_barrier_semaphore()
-    near = [device(dx=dx, dc=dc) for dx, dc in row_steps]
-    near += [device(dy=dy) for dy in (2, 1, 3)]
-    near += [device(dz=dz) for dz in (2, -2, 1, -1)]
+    near = [device(dz=dz) for dz in (2, -2)] + [device(dy=2)]
+    near += [device(dx=dx, dc=dc) for dx, dc in row_steps]
+    near += [device(dy=dy) for dy in (1, 3)]
+    near += [device(dz=dz) for dz in (1, -1)]
     for to in near:
         pl.semaphore_signal(barrier, inc=1, device_id=to, device_id_type=MESH)
 
@@ -132,9 +142,8 @@
         idf[...].astype(F32).astype(BF16), spread, (((0,), (0,)), ((), ())),
         preferred_element_type=F32,
     ).astype(BF16)
-    tot[0] = totals + jnp.dot(mine, table, preferred_element_type=F32)
+    tot[0:TROWS] = (totals + jnp.dot(mine, table, preferred_element_type=F32))[:TROWS]
     back[...] = jnp.zeros_like(back)
-    exb[...] = jnp.zeros_like(exb)
 
     pl.semaphore_wait(barrier, len(near))
 
@@ -150,41 +159,43 @@
     def place(slot):
         return slot // 2 + (slot % 2) * (NZ // 2)
 
-    def pass_rows(slot, chunk):
-        return pas.at[place(slot), pl.ds(chunk * (PTOK // CHUNKS), PTOK // CHUNKS)]
-
-    def pass_recv(slot, chunk):
+    def pass_recv(slot):
         if slot % 2:
             return odd_recv
-        return end_recv if slot == NZ // 2 else relay_recv.at[place(slot) * CHUNKS + chunk]
+        return end_recv if slot == NZ // 2 else relay_recv.at[(slot % (NZ // 2)) // 2 - 1 + 3 * (slot // (NZ // 2))]
 
     def relay(entry):
         source, hops = entry
-        for chunk in range(CHUNKS):
-            if source:
-                arrive(pass_rows(source, chunk), pass_recv(source, chunk))
-            for dz, slot in hops:
-                remote(
-                    pass_rows(source, chunk), pass_rows(slot, chunk),
-                    pas_send, pass_recv(slot, chunk), device(dz=dz),
-                ).start()
-
-    sent = pl.ds(0, NCLUS + 1)
+        if source:
+            arrive(pas.at[place(source)], pass_recv(source))
+        for dz, slot in hops:
+            remote(
+                pas.at[place(source)], pas.at[place(slot)],
+                pas_send, pass_recv(slot), device(dz=dz),
+            ).start()
+
+    for dy in (2, 1, 3):
+        pl.semaphore_signal(plane_sem, inc=1, device_id=device(dy=dy), device_id_type=MESH)
+
+    def rows_of(slot, count=1):
+        return pl.ds(slot * TROWS, count * TROWS)
+
+    def tot_send_to(dy, dx, dc):
+        slot = dy * ROW + dx * NC + dc
+        remote(
+            tot.at[rows_of(0)], tot.at[rows_of(slot)], tot_send, tot_recv,
+            device(dy=dy, dx=dx, dc=dc),
+        ).start()
+
     for dx, dc in row_steps:
-        slot = dx * NC + dc
-        remote(
-            tot.at[0, sent], tot.at[slot, sent], tot_send, row_tot_recv.at[slot], device(dx=dx, dc=dc)
-        ).start()
-
-    def col_send(slot):
-        for dy in (2, 1, 3):
-            remote(
-                tot.at[slot, sent], tot.at[dy * ROW + slot, sent],
-                tot_send, col_tot_recv, device(dy=dy),
-            ).start()
-
-    col_send(0)
+        tot_send_to(0, dx, dc)
+    for dy in (2, 1, 3):
+        tot_send_to(dy, 0, 0)
     relay(RELAYS[0])
+    pl.semaphore_wait(plane_sem, 3)
+    for dy, dx, dc in OFFSETS:
+        if dy and (dx or dc):
+            tot_send_to(dy, dx, dc)
     loads[4].wait()
     loads[5].wait()
     turn = lax.rem(iota((NZ, NZ * ROW), 0) + z, NZ) * ROW + (x * NC + core)
@@ -201,19 +212,15 @@
     counts = jnp.zeros((NZ, PLANE), F32)
     for k in range(FB):
         counts += jnp.where(jnp.abs(slot_id - ids[:, k : k + 1]) < 0.5, 1.0, 0.0)
-    up = jnp.where(lax.div(iota((EXP, NZ), 0), CPAD) == iota((EXP, NZ), 1), 1.0, 0.0).astype(BF16)
-    over = jnp.where(
-        lax.div(iota((PLANE, EROWS), 1), CPAD) == iota((PLANE, EROWS), 0), 1.0, 0.0
-    ).astype(BF16)
+    up = jnp.where(tenth(iota((EXP, NZ), 0)) == iota((EXP, NZ), 1), 1.0, 0.0).astype(BF16)
+    wide_shape = (PLANE, PLANE * TROWS)
+    over = jnp.where(eleventh(iota(wide_shape, 1)) == iota(wide_shape, 0), 1.0, 0.0).astype(BF16)
     tall = jnp.dot(up, counts.astype(BF16), preferred_element_type=F32).astype(BF16)
     counts = jnp.dot(tall, over, preferred_element_type=F32)
-    same = lax.rem(iota((EXP, EROWS), 0), CPAD) == lax.rem(iota((EXP, EROWS), 1), CPAD)
+    to, at = iota((EXP, PLANE * TROWS), 0), iota((EXP, PLANE * TROWS), 1)
+    same = to - NCLUS * tenth(to) == at - TROWS * eleventh(at)
     mix[...] = jnp.where(same, counts, 0.0).astype(BF16)
 
-    for dx, dc in row_steps:
-        slot = dx * NC + dc
-        arrive(tot.at[slot, sent], row_tot_recv.at[slot])
-        col_send(slot)
     for dx, dc in row_steps:
         slot = dx * NC + dc
         remote(
@@ -224,19 +231,18 @@
         pl.semaphore_signal(far_sem, inc=1, device_id=device(dz=dz), device_id_type=MESH)
     relay(RELAYS[1])
     relay(RELAYS[2])
-    arrive(tot.at[pl.ds(ROW, PLANE - ROW), sent], col_tot_recv)
-
-    table = jnp.where(iota((PLANE, CPAD, D), 1) < NCLUS, tot[...], 0.0).reshape(EROWS, D)
+    arrive(tot.at[rows_of(1, PLANE - 1)], tot_recv)
+
     counts = mix[...]
     summed = None
-    for piece in split3(table):
+    for piece in split3(tot[...]):
         term = jnp.dot(counts, piece, preferred_element_type=F32)
         summed = term if summed is None else summed + term
-    part[...] = summed.reshape(NZ, CPAD, D)
+    part[...] = summed
     pl.semaphore_wait(far_sem, 2)
     for dz in RS_ORDER:
         remote(
-            part.at[dz, pl.ds(0, NCLUS)], rs.at[dz, pl.ds(0, NCLUS)],
+            part.at[pl.ds(dz * NCLUS, NCLUS)], rs.at[dz, pl.ds(0, NCLUS)],
             rs_send, rs_recv, device(dz=dz),
         ).start()
     arrive(qbuf.at[pl.ds(1, ROW - 1)], row_query_recv)
@@ -246,12 +252,11 @@
             query_send, col_query_recv, device(dy=dy),
         ).start()
 
-    owner = lax.div(iota((PLANE, EROWS), 1), CPAD)
-    spread = jnp.where(
-        lax.rem(iota((D, EROWS), 1), CPAD) == iota((D, EROWS), 0), 1.0, 0.0
-    ).astype(BF16)
-    idf_rows = tot[:, NCLUS].astype(BF16)
+    lanes = iota((D, EROWS), 1)
+    spread = jnp.where(lanes - NCLUS * tenth(lanes) == iota((D, EROWS), 0), 1.0, 0.0).astype(BF16)
+    idf_rows = tot[pl.ds(NCLUS, PLANE, stride=TROWS), :].astype(BF16)
     idf_rows = jnp.dot(idf_rows, spread, preferred_element_type=F32)
+    owner = tenth(iota((PLANE, EROWS), 1))
     exp_weight = jnp.where(owner == iota((PLANE, EROWS), 0), idf_rows, 0.0).astype(BF16)
     query_weight = jnp.where(
         lax.div(iota((PLANE, QROWS), 1), QTOK) == iota((PLANE, QROWS), 0), 1.0, 0.0
@@ -261,15 +266,15 @@
         relay(entry)
 
     arrive(rs.at[pl.ds(1, NZ - 1), pl.ds(0, NCLUS)], rs_recv)
-    rows = part[0, 0:NCLUS]
+    rows = part[0:NCLUS]
     for dz in range(1, NZ):
         rows += rs[dz, 0:NCLUS]
     factor = lax.rsqrt(jnp.mean(rows * rows, axis=1, keepdims=True) + 1e-06)
-    exb[0, 0:NCLUS] = (rows * factor).astype(BF16)
+    exb[0:NCLUS] = (rows * factor).astype(BF16)
     for dy, dx, dc in OFFSETS:
         slot = dy * ROW + dx * NC + dc
         remote(
-            exb.at[0, pl.ds(0, NCLUS)], exb.at[slot, pl.ds(0, NCLUS)], exp_send, exp_recv,
+            exb.at[pl.ds(0, NCLUS)], exb.at[pl.ds(slot * NCLUS, NCLUS)], exp_send, exp_recv,
             device(dy=dy, dx=dx, dc=dc),
         ).start()
 
@@ -277,14 +282,17 @@
     arrive(pas.at[pl.ds(NZ // 2, NZ // 2)], odd_recv)
     arrive(pas.at[NZ // 4], end_recv)
 
-    def maxima(vectors, n):
-        scores = lax.dot_general(pas[n], vectors, NT, preferred_element_type=F32)
-        return jnp.max(scores, axis=0, keepdims=True)
+    def score(vectors, out, at):
+        for n in range(0, NZ, GROUP):
+            tokens = pas[n : n + GROUP].reshape(GROUP * PTOK, D)
+            scores = lax.dot_general(tokens, vectors, NT, preferred_element_type=F32)
+            for m in range(GROUP):
+                top = jnp.max(scores[m * PTOK : (m + 1) * PTOK], axis=0, keepdims=True)
+                out[n + m : n + m + 1, at : at + vectors.shape[0]] = top
 
     for tile in range(QROWS // TILE):
         vectors = qbuf[tile * ROW : (tile + 1) * ROW].reshape(TILE, D)
-        for n in range(NZ):
-            best[n : n + 1, tile * TILE : (tile + 1) * TILE] = maxima(vectors, n)
+        score(vectors, best, tile * TILE)
 
     def reduce(weight, values):
         hi, mid, low = split3(values)
@@ -292,7 +300,7 @@
         total += lax.dot_general(weight, mid, NT, preferred_element_type=F32)
         return total + lax.dot_general(weight, low, NT, preferred_element_type=F32)
 
-    plain = reduce(query_weight, best[:, :QROWS]) * (1.0 / QTOK)
+    plain = reduce(query_weight, best[...]) * (1.0 / QTOK)
     back[:, 0:NZ] = plain
 
     ids = cand[...]
@@ -310,14 +318,10 @@
     slot_hot = jnp.where(iota((PLANE, NCAND), 0) == cand_slot, 1.0, 0.0).astype(BF16)
     n_hot = iota((NZ, NCAND), 0) == cand_n
 
-    arrive(exb.at[pl.ds(1, PLANE - 1), pl.ds(0, NCLUS)], exp_recv)
-    for tile in range(EROWS // TILE):
-        part_rows = TILE // CPAD
-        vectors = exb[tile * part_rows : (tile + 1) * part_rows].reshape(TILE, D)
-        for n in range(NZ):
-            at = QROWS + tile * TILE
-            best[n : n + 1, at : at + TILE] = maxima(vectors, n)
-    added = reduce(exp_weight, best[:, QROWS:]) * (1.0 / (8.0 * NCLUS))
+    arrive(exb.at[pl.ds(NCLUS, EROWS - NCLUS)], exp_recv)
+    for at in range(0, EROWS, TILE):
+        score(exb[at : min(at + TILE, EROWS)], best_exp, at)
+    added = reduce(exp_weight, best_exp[...]) * (1.0 / (8.0 * NCLUS))
     back[:, NZ : 2 * NZ] = plain + added
 
     for dy, dx, dc in OFFSETS:
@@ -328,11 +332,11 @@
         ).start()
     ret[0:1, :] = back[0:1, :]
     others = pl.ds(1, PLANE - 1)
-    leave(tot.at[others, sent], tot_send)
+    leave(tot.at[rows_of(1, PLANE - 1)], tot_send)
     leave(qbuf.at[others], query_send)
     leave(pas.at[pl.ds(1, NZ - 1)], pas_send)
     leave(rs.at[pl.ds(1, NZ - 1), pl.ds(0, NCLUS)], rs_send)
-    leave(exb.at[others, pl.ds(0, NCLUS)], exp_send)
+    leave(exb.at[pl.ds(NCLUS, EROWS - NCLUS)], exp_send)
     arrive(ret.at[others], ret_recv)
     flat = ret[...].T[: 2 * NZ, :]
     chosen = None
@@ -349,7 +353,7 @@
     anywhere = pl.BlockSpec(memory_space=pl.ANY)
     scores = pl.pallas_call(
         kernel,
-        out_shape=jax.ShapeDtypeStruct((2, NCAND), F32),
+        out_shape=pltpu.VMEM((2, NCAND), F32),
         in_specs=[anywhere] * 7,
         out_specs=pl.BlockSpec(memory_space=pltpu.VMEM),
         scratch_shapes=[
@@ -361,21 +365,23 @@
             pltpu.VMEM((1, NCAND), jnp.int32),
             pltpu.VMEM((FB, NZ * ROW), jnp.int32),
             pltpu.VMEM((NCLUS, NZ * ROW), jnp.int32),
-            pltpu.VMEM((PLANE, CPAD, D), F32),
-            pltpu.VMEM((EXP, EROWS), BF16),
+            pltpu.VMEM((PLANE * TROWS, D), F32),
+            pltpu.VMEM((EXP, PLANE * TROWS), BF16),
+            pltpu.VMEM((EXP, D), F32),
             pltpu.VMEM((NZ, CPAD, D), F32),
-            pltpu.VMEM((NZ, CPAD, D), F32),
-            pltpu.VMEM((PLANE, CPAD, D), BF16),
-            pltpu.VMEM((NZ, QROWS + EROWS), F32),
+            pltpu.VMEM((EROWS, D), BF16),
+            pltpu.VMEM((NZ, QROWS), F32),
+            pltpu.VMEM((NZ, EROWS), F32),
             pltpu.VMEM((PLANE, D), F32),
             pltpu.VMEM((PLANE, D), F32),
             dma((7,)),
-            dma, dma((ROW,)), dma,
+            dma, dma,
             dma, dma, dma,
-            dma, dma((NZ * CHUNKS // 2,)), dma, dma,
+            dma, dma((6,)), dma, dma,
             dma, dma,
             dma, dma,
             dma, dma,
+            pltpu.SemaphoreType.REGULAR,
             pltpu.SemaphoreType.REGULAR,
             pltpu.SemaphoreType.REGULAR,
         ],

time: 43.7 us -> 41.2 us (0.943)
  Pallas kernels: 41.5 us -> 39.8 us
  local copies, waits for them, and re-layouts: 1.32 us -> 0.57 us
    pallas_call x1, Pallas kernels: 41.5 us -> 39.8 us  [local(): pl.pallas_call(kernel, out_shape=pltpu.VMEM((2, NCAND), F32), in_specs=[a...]
    slice x1, local copies, waits for them, and re-layouts: 1.32 us -> 0.57 us  [local(): return (scores[0:1], scores[1:2])]
where the time goes in v3:
time: 41.2 us; the launch traced here: 41 us
  Pallas kernels  39.8 us (97%)
  between operations  0.64 us (2%)
  local copies, waits for them, and re-layouts  0.57 us (1%)
    pallas_call x1, Pallas kernels, local(): pl.pallas_call(kernel, out_shape=pltpu.VMEM((2, NCAND), F32), in_specs=[a...  39.8 us

profile of v3, /device:TPU:1, one launch (start us, length us, event | category | flops | bytes accessed | tf_op | source)
XLA Modules:
  0.0 41.0 jit_solution(12610527083171790989)
XLA Ops:
  0.6 39.8 %shard_map.86 = f32[2,256]{1,0:T(2,128)S(1)} custom-call(bf16[1,32,128]{2,1,0:T(8,128)(2,1)} %q_hbm.1, bf16[1,128,128]{2,1,0:T(8,128)(2,1)} %p_hbm.1, s32[4,128]{1,0:T(4,128)} %lab_hbm.1, s32[4]{0:T(128)} %len_hbm.1, s32[1,256]{1,0:T(1,128)} %cand_hbm.1, s32[3,128]{1,0:T(4,128)} %bitcast.3, s32[10,128]{1,0:T(8,128)} %bitcast.2), custom_call_target="tpu_custom_call" | custom-call | tf_op jit(solution)/shard_map/pallas_call | solution.py:354
  40.5 0.6 %fusion = (f32[1,256]{1,0:T(1,128)}, f32[1,256]{1,0:T(1,128)}) fusion(f32[2,256]{1,0:T(2,128)S(1)} %shard_map.86), kind=kLoop, calls=%fused_computation | loop fusion | bytes 4096 | tf_op jit(solution)/shard_map/slice | solution.py:390

commit v4 on v3

--- a/solution.py
+++ b/solution.py
@@ -24,16 +24,20 @@
 EXP = NZ * NCLUS
 TILE = 256
 GROUP = 4
-RS_ORDER = (8, 7, 9, 6, 10, 5, 11, 4, 12, 3, 13, 2, 14, 1, 15)
+LATE_RELAYS = 3
 RELAYS = (
     (0, ((2, 2), (-2, 14), (1, 1), (-1, 15))),
     (2, ((2, 4), (1, 3))),
     (14, ((-2, 12), (-1, 13))),
     (4, ((2, 6), (1, 5))),
     (12, ((-2, 10), (-1, 11))),
-    (6, ((2, 8), (1, 7))),
-    (10, ((-1, 9),)),
+    (6, ((1, 7),)),
+    (10, ((-2, 8), (-1, 9))),
 )
+
+RELAYED = [source for source, _ in RELAYS]
+PLACES = RELAYED + [1, 15, 3, 13, 5, 11, 7, 9, 8]
+HELD, LAST = len(RELAYED), NZ - 3
 
 
 def ring(n):
@@ -71,7 +75,7 @@
     out_ref,
     len_ref, qbuf, praw, pas, lab, cand, fb, idf, tot, mix, part, rs, exb, best, best_exp, back, ret,
     load_sem, tot_send, tot_recv, query_send, row_query_recv, col_query_recv,
-    pas_send, relay_recv, odd_recv, end_recv, rs_send, rs_recv, exp_send, exp_recv, ret_send, ret_recv, near_sem, far_sem, plane_sem,
+    pas_send, relay_recv, rest_recv, rs_send, rs_recv, exp_send, exp_recv, ret_send, ret_recv, near_sem, far_sem, plane_sem,
 ):
     s = lax.axis_index("shard")
     y = lax.axis_index("rep")
@@ -157,12 +161,11 @@
         pl.semaphore_signal(near_sem, inc=1, device_id=device(dz=dz), device_id_type=MESH)
 
     def place(slot):
-        return slot // 2 + (slot % 2) * (NZ // 2)
+        return PLACES.index(slot)
 
     def pass_recv(slot):
-        if slot % 2:
-            return odd_recv
-        return end_recv if slot == NZ // 2 else relay_recv.at[(slot % (NZ // 2)) // 2 - 1 + 3 * (slot // (NZ // 2))]
+        at = place(slot)
+        return relay_recv.at[at] if at < HELD else rest_recv.at[at // LAST]
 
     def relay(entry):
         source, hops = entry
@@ -229,8 +232,8 @@
     pl.semaphore_wait(near_sem, 2)
     for dz in (4, -4):
         pl.semaphore_signal(far_sem, inc=1, device_id=device(dz=dz), device_id_type=MESH)
-    relay(RELAYS[1])
-    relay(RELAYS[2])
+    for entry in RELAYS[1:LATE_RELAYS]:
+        relay(entry)
     arrive(tot.at[rows_of(1, PLANE - 1)], tot_recv)
 
     counts = mix[...]
@@ -238,11 +241,14 @@
     for piece in split3(tot[...]):
         term = jnp.dot(counts, piece, preferred_element_type=F32)
         summed = term if summed is None else summed + term
-    part[...] = summed
+    for dz in range(NZ):
+        part[dz, 0:NCLUS] = summed[dz * NCLUS : (dz + 1) * NCLUS]
     pl.semaphore_wait(far_sem, 2)
-    for dz in RS_ORDER:
-        remote(
-            part.at[pl.ds(dz * NCLUS, NCLUS)], rs.at[dz, pl.ds(0, NCLUS)],
+    for k in range(NZ - 1):
+        target = k + lax.div(k + NZ - z, NZ)
+        dz = lax.rem(target + NZ - z, NZ)
+        remote(
+            part.at[dz, pl.ds(0, NCLUS)], rs.at[dz, pl.ds(0, NCLUS)],
             rs_send, rs_recv, device(dz=dz),
         ).start()
     arrive(qbuf.at[pl.ds(1, ROW - 1)], row_query_recv)
@@ -262,11 +268,11 @@
         lax.div(iota((PLANE, QROWS), 1), QTOK) == iota((PLANE, QROWS), 0), 1.0, 0.0
     ).astype(BF16)
 
-    for entry in RELAYS[3:]:
+    for entry in RELAYS[LATE_RELAYS:]:
         relay(entry)
 
     arrive(rs.at[pl.ds(1, NZ - 1), pl.ds(0, NCLUS)], rs_recv)
-    rows = part[0:NCLUS]
+    rows = part[0, 0:NCLUS]
     for dz in range(1, NZ):
         rows += rs[dz, 0:NCLUS]
     factor = lax.rsqrt(jnp.mean(rows * rows, axis=1, keepdims=True) + 1e-06)
@@ -279,20 +285,25 @@
         ).start()
 
     arrive(qbuf.at[pl.ds(ROW, PLANE - ROW)], col_query_recv)
-    arrive(pas.at[pl.ds(NZ // 2, NZ // 2)], odd_recv)
-    arrive(pas.at[NZ // 4], end_recv)
-
-    def score(vectors, out, at):
-        for n in range(0, NZ, GROUP):
-            tokens = pas[n : n + GROUP].reshape(GROUP * PTOK, D)
+    def score(vectors, out, at, first, last):
+        for n in range(first, last, GROUP):
+            stop = min(n + GROUP, last)
+            tokens = pas[n:stop].reshape((stop - n) * PTOK, D)
             scores = lax.dot_general(tokens, vectors, NT, preferred_element_type=F32)
-            for m in range(GROUP):
-                top = jnp.max(scores[m * PTOK : (m + 1) * PTOK], axis=0, keepdims=True)
-                out[n + m : n + m + 1, at : at + vectors.shape[0]] = top
-
-    for tile in range(QROWS // TILE):
-        vectors = qbuf[tile * ROW : (tile + 1) * ROW].reshape(TILE, D)
-        score(vectors, best, tile * TILE)
+            for m in range(n, stop):
+                top = scores[(m - n) * PTOK : (m - n + 1) * PTOK]
+                out[m : m + 1, at : at + vectors.shape[0]] = jnp.max(top, axis=0, keepdims=True)
+
+    def plain_score(first, last):
+        for tile in range(QROWS // TILE):
+            vectors = qbuf[tile * ROW : (tile + 1) * ROW].reshape(TILE, D)
+            score(vectors, best, tile * TILE, first, last)
+
+    plain_score(0, HELD)
+    arrive(pas.at[pl.ds(HELD, LAST - HELD)], rest_recv.at[0])
+    plain_score(HELD, LAST)
+    arrive(pas.at[pl.ds(LAST, NZ - LAST)], rest_recv.at[1])
+    plain_score(LAST, NZ)
 
     def reduce(weight, values):
         hi, mid, low = split3(values)
@@ -314,13 +325,16 @@
         + lax.rem(cand_c + core, 2)
     )
     cand_n = lax.rem(z + NZ - cand_z, NZ)
-    cand_n = lax.div(cand_n, 2) + lax.rem(cand_n, 2) * (NZ // 2)
     slot_hot = jnp.where(iota((PLANE, NCAND), 0) == cand_slot, 1.0, 0.0).astype(BF16)
-    n_hot = iota((NZ, NCAND), 0) == cand_n
+    held = iota((NZ, NCAND), 0)
+    slot_at = jnp.zeros((NZ, NCAND), jnp.int32)
+    for at, slot in enumerate(PLACES):
+        slot_at = jnp.where(held == at, slot, slot_at)
+    n_hot = slot_at == cand_n
 
     arrive(exb.at[pl.ds(NCLUS, EROWS - NCLUS)], exp_recv)
     for at in range(0, EROWS, TILE):
-        score(exb[at : min(at + TILE, EROWS)], best_exp, at)
+        score(exb[at : min(at + TILE, EROWS)], best_exp, at, 0, NZ)
     added = reduce(exp_weight, best_exp[...]) * (1.0 / (8.0 * NCLUS))
     back[:, NZ : 2 * NZ] = plain + added
 
@@ -367,7 +381,7 @@
             pltpu.VMEM((NCLUS, NZ * ROW), jnp.int32),
             pltpu.VMEM((PLANE * TROWS, D), F32),
             pltpu.VMEM((EXP, PLANE * TROWS), BF16),
-            pltpu.VMEM((EXP, D), F32),
+            pltpu.VMEM((NZ, CPAD, D), F32),
             pltpu.VMEM((NZ, CPAD, D), F32),
             pltpu.VMEM((EROWS, D), BF16),
             pltpu.VMEM((NZ, QROWS), F32),
@@ -377,7 +391,7 @@
             dma((7,)),
             dma, dma,
             dma, dma, dma,
-            dma, dma((6,)), dma, dma,
+            dma, dma((HELD,)), dma((2,)),
             dma, dma,
             dma, dma,
             dma, dma,

time: 41.2 us -> 40.7 us (0.988)
  Pallas kernels: 39.8 us -> 39.3 us
    pallas_call x1, Pallas kernels: 39.8 us -> 39.3 us  [local(): pl.pallas_call(kernel, out_shape=pltpu.VMEM((2, NCAND), F32), in_specs=[a...]
where the time goes in v4:
time: 40.7 us; the launch traced here: 40.5 us
  Pallas kernels  39.3 us (97%)
  between operations  0.64 us (2%)
  local copies, waits for them, and re-layouts  0.57 us (1%)
    pallas_call x1, Pallas kernels, local(): pl.pallas_call(kernel, out_shape=pltpu.VMEM((2, NCAND), F32), in_specs=[a...  39.3 us

profile of v4, /device:TPU:1, one launch (start us, length us, event | category | flops | bytes accessed | tf_op | source)
XLA Modules:
  0.0 40.5 jit_solution(18337644360310767998)
XLA Ops:
  0.6 39.3 %shard_map.86 = f32[2,256]{1,0:T(2,128)S(1)} custom-call(bf16[1,32,128]{2,1,0:T(8,128)(2,1)} %q_hbm.1, bf16[1,128,128]{2,1,0:T(8,128)(2,1)} %p_hbm.1, s32[4,128]{1,0:T(4,128)} %lab_hbm.1, s32[4]{0:T(128)} %len_hbm.1, s32[1,256]{1,0:T(1,128)} %cand_hbm.1, s32[3,128]{1,0:T(4,128)} %bitcast.3, s32[10,128]{1,0:T(8,128)} %bitcast.2), custom_call_target="tpu_custom_call" | custom-call | tf_op jit(solution)/shard_map/pallas_call | solution.py:368
  39.9 0.6 %fusion = (f32[1,256]{1,0:T(1,128)}, f32[1,256]{1,0:T(1,128)}) fusion(f32[2,256]{1,0:T(2,128)S(1)} %shard_map.86), kind=kLoop, calls=%fused_computation | loop fusion | bytes 4096 | tf_op jit(solution)/shard_map/slice | solution.py:404

commit v5 on v4

--- a/solution.py
+++ b/solution.py
@@ -23,8 +23,9 @@
 EROWS = PLANE * NCLUS
 EXP = NZ * NCLUS
 TILE = 256
-GROUP = 4
+GROUP = 8
 LATE_RELAYS = 3
+FIRST = 8
 RELAYS = (
     (0, ((2, 2), (-2, 14), (1, 1), (-1, 15))),
     (2, ((2, 4), (1, 3))),
@@ -244,13 +245,16 @@
     for dz in range(NZ):
         part[dz, 0:NCLUS] = summed[dz * NCLUS : (dz + 1) * NCLUS]
     pl.semaphore_wait(far_sem, 2)
-    for k in range(NZ - 1):
+    def sum_send(k):
         target = k + lax.div(k + NZ - z, NZ)
         dz = lax.rem(target + NZ - z, NZ)
         remote(
             part.at[dz, pl.ds(0, NCLUS)], rs.at[dz, pl.ds(0, NCLUS)],
             rs_send, rs_recv, device(dz=dz),
         ).start()
+
+    for k in range(FIRST):
+        sum_send(k)
     arrive(qbuf.at[pl.ds(1, ROW - 1)], row_query_recv)
     for dy in (2, 1, 3):
         remote(
@@ -268,7 +272,11 @@
         lax.div(iota((PLANE, QROWS), 1), QTOK) == iota((PLANE, QROWS), 0), 1.0, 0.0
     ).astype(BF16)
 
-    for entry in RELAYS[LATE_RELAYS:]:
+    for entry in RELAYS[LATE_RELAYS : LATE_RELAYS + 2]:
+        relay(entry)
+    for k in range(FIRST, NZ - 1):
+        sum_send(k)
+    for entry in RELAYS[LATE_RELAYS + 2 :]:
         relay(entry)
 
     arrive(rs.at[pl.ds(1, NZ - 1), pl.ds(0, NCLUS)], rs_recv)

time: 40.7 us -> 40.4 us (level)
  no operation moved by 1% of the time
where the time goes in v5:
time: 40.4 us; the launch traced here: 40.2 us
  Pallas kernels  39 us (97%)
  between operations  0.64 us (2%)
  local copies, waits for them, and re-layouts  0.57 us (1%)
    pallas_call x1, Pallas kernels, local(): pl.pallas_call(kernel, out_shape=pltpu.VMEM((2, NCAND), F32), in_specs=[a...  39 us

profile of v5, /device:TPU:1, one launch (start us, length us, event | category | flops | bytes accessed | tf_op | source)
XLA Modules:
  0.0 40.2 jit_solution(1193894959351403156)
XLA Ops:
  0.6 39.0 %shard_map.86 = f32[2,256]{1,0:T(2,128)S(1)} custom-call(bf16[1,32,128]{2,1,0:T(8,128)(2,1)} %q_hbm.1, bf16[1,128,128]{2,1,0:T(8,128)(2,1)} %p_hbm.1, s32[4,128]{1,0:T(4,128)} %lab_hbm.1, s32[4]{0:T(128)} %len_hbm.1, s32[1,256]{1,0:T(1,128)} %cand_hbm.1, s32[3,128]{1,0:T(4,128)} %bitcast.3, s32[10,128]{1,0:T(8,128)} %bitcast.2), custom_call_target="tpu_custom_call" | custom-call | tf_op jit(solution)/shard_map/pallas_call | solution.py:376
  39.6 0.6 %fusion = (f32[1,256]{1,0:T(1,128)}, f32[1,256]{1,0:T(1,128)}) fusion(f32[2,256]{1,0:T(2,128)S(1)} %shard_map.86), kind=kLoop, calls=%fused_computation | loop fusion | bytes 4096 | tf_op jit(solution)/shard_map/slice | solution.py:412
